TPU v7x, 256 devices: a whole 4x4x8 slice. The times are simulated.
256 devices in a mesh: row: 32 (over y, z_lo, x), col: 8 (over z_hi, core).
Axes of the slice: x: 4, y: 4, z: 8 (z_hi: 4, z_lo: 2; z = z_hi * 2 + z_lo), core: 2. Of those that a mesh axis runs over, the one named last changes fastest.
Arguments:
- p_cov: float32 [8192, 8192], P('row', 'col'), as said below
- a_blocks: float32 [64, 16, 128, 128], P('row'), may hold values from -0.15625 to 0.15625
- pattern: int32 [64, 16], P('row'), may hold values from -1 to 63, as said below
- q_diag: float32 [8192], P('row'), may hold values from 0.2 to 2
Outputs:
- p_next: float32 [8192, 8192], P('row', 'col')
Inputs may be any that keep to these rules, and one draw needn't show every extreme that they name: p_cov is exactly symmetric. `pattern`: in each row i the entries that are not -1 are distinct, lie within 8 of i, include i itself and fill the leading slots; some row uses all 16 slots.
All inputs are finite; a program needn't handle non-finite values.
Results may differ from a plain program's by a relative error of at most 0.0003.
Values sent between devices are 32-bit elements; how exact they have to be, the bound alone decides.
A program may use at most 64 MiB of HBM per device.

v0:
```python
import jax
import jax.numpy as jnp
from jax import lax
from jax.sharding import PartitionSpec as P

BS = 128
REACH = 8


time_step = 0.25


def shifted(array, axis, by):
    peers = lax.axis_size(axis)
    pairs = [(i, i + by) for i in range(peers) if 0 <= i + by < peers]
    return lax.ppermute(array, axis, pairs)


def band_matrix(blocks, slots, first_block, extent):
    picks = jnp.arange(extent, dtype=jnp.int32)[None, None, :]
    onehot = ((slots - first_block)[:, :, None] == picks).astype(jnp.float32)
    banded = jnp.einsum("bse,bsxy->bxey", onehot, blocks, precision=lax.Precision.HIGHEST)
    return banded.reshape(blocks.shape[0] * BS, extent * BS)


def body(p_cov, a_blocks, pattern, q_diag):
    rows_dev, cols_dev = p_cov.shape
    row_count = lax.axis_size("row")
    col_count = lax.axis_size("col")
    row_idx = lax.axis_index("row")
    col_idx = lax.axis_index("col")
    row_blocks = rows_dev // BS
    span_devs = REACH * BS // rows_dev
    group_rows = row_count // col_count
    global_rows = row_idx * rows_dev + jnp.arange(rows_dev, dtype=jnp.int32)[:, None]
    global_cols = col_idx * cols_dev + jnp.arange(cols_dev, dtype=jnp.int32)[None, :]
    noise_term = jnp.where(global_rows == global_cols, q_diag[:, None], 0.0)
    row_band = band_matrix(
        a_blocks,
        pattern,
        row_idx * row_blocks - span_devs * row_blocks,
        (2 * span_devs + 1) * row_blocks,
    )

    def forward(p_local):
        pieces = []
        for offset in range(-span_devs, span_devs + 1):
            if offset == 0:
                pieces.append(p_local)
            else:
                pieces.append(shifted(p_local, "row", -offset))
        extended = jnp.concatenate(pieces, axis=0)
        return jnp.dot(
            row_band, extended, precision=lax.Precision.HIGHEST, preferred_element_type=jnp.float32
        )

    def mirrored(product):
        part_len = rows_dev // col_count
        moved = product.reshape(col_count, part_len, cols_dev)
        moved = lax.all_to_all(moved, "col", split_axis=0, concat_axis=0, tiled=True)
        moved = (
            moved.reshape(col_count, part_len, group_rows, rows_dev)
            .transpose(0, 2, 1, 3)
            .reshape(row_count, part_len, rows_dev)
        )
        moved = lax.all_to_all(moved, "row", split_axis=0, concat_axis=0, tiled=True)
        moved = moved.reshape(col_count, group_rows, part_len, rows_dev)
        moved = lax.all_to_all(moved, "col", split_axis=0, concat_axis=0, tiled=True)
        return moved.transpose(3, 1, 0, 2).reshape(rows_dev, cols_dev)

    def tendency(p_local):
        product = forward(p_local)
        other = mirrored(product)
        return product + other + noise_term

    k_first = tendency(p_cov)
    p_mid = p_cov + time_step * k_first
    k_second = tendency(p_mid)
    return p_cov + 0.5 * time_step * (k_first + k_second)


def solution(mesh):
    return jax.shard_map(
        body,
        mesh=mesh,
        in_specs=(P("row", "col"), P("row", None, None, None), P("row", None), P("row")),
        out_specs=P("row", "col"),
        check_vma=False,
    )
```

profile of v0, /device:TPU:27, one launch (start us, length us, event | category | flops | bytes accessed | tf_op | source)
XLA Modules:
  0.0 526.9 jit_solution(5646958410858572032)
XLA Ops:
  0.0 3.8 collective-permute-start
  5.7 3.8 collective-permute-start.2
  15.5 11.9 %collective-permute-done = f32[256,1024]{1,0:T(8,128)} collective-permute-done((f32[256,1024]{1,0:T(8,128)}, f32[256,1024]{1,0:T(8,128)}, u32[]{:S(2)}, u32[]{:S(2)}) %collective-permute-start) | collective-permute-done | bytes 1048608 | tf_op jit(solution)/shard_map/ppermute | solution.py:16
  27.4 4.4 collective-permute-start.5
  31.8 19.1 %collective-permute-done.1 = f32[256,1024]{1,0:T(8,128)} collective-permute-done((f32[256,1024]{1,0:T(8,128)}, f32[256,1024]{1,0:T(8,128)}, u32[]{:S(2)}, u32[]{:S(2)}) %collective-permute-start.1) | collective-permute-done | bytes 1048608 | tf_op jit(solution)/shard_map/ppermute | solution.py:16
  50.9 3.5 collective-permute-start.6
  57.0 19.4 %collective-permute-done.2 = f32[256,1024]{1,0:T(8,128)} collective-permute-done((f32[256,1024]{1,0:T(8,128)}, f32[256,1024]{1,0:T(8,128)}, u32[]{:S(2)}, u32[]{:S(2)}) %collective-permute-start.2) | collective-permute-done | bytes 1048608 | tf_op jit(solution)/shard_map/ppermute | solution.py:16
  76.4 4.2 collective-permute-start.7
  86.1 12.8 %collective-permute-done.4 = f32[256,1024]{1,0:T(8,128)} collective-permute-done((f32[256,1024]{1,0:T(8,128)}, f32[256,1024]{1,0:T(8,128)}, u32[]{:S(2)}, u32[]{:S(2)}) %collective-permute-start.4) | collective-permute-done | bytes 1048608 | tf_op jit(solution)/shard_map/ppermute | solution.py:16
  100.3 20.9 %collective-permute-done.6 = f32[256,1024]{1,0:T(8,128)S(1)} collective-permute-done((f32[256,1024]{1,0:T(8,128)}, f32[256,1024]{1,0:T(8,128)S(1)}, u32[]{:S(2)}, u32[]{:S(2)}) %collective-permute-start.6) | collective-permute-done | bytes 1048608 | tf_op jit(solution)/shard_map/ppermute | solution.py:16
  121.3 14.8 %collective-permute-done.7 = f32[256,1024]{1,0:T(8,128)S(1)} collective-permute-done((f32[256,1024]{1,0:T(8,128)}, f32[256,1024]{1,0:T(8,128)S(1)}, u32[]{:S(2)}, u32[]{:S(2)}) %collective-permute-start.7) | collective-permute-done | bytes 1048608 | tf_op jit(solution)/shard_map/ppermute | solution.py:16
  136.3 8.2 %fusion = f32[256,1024]{1,0:T(8,128)S(1)} fusion(f32[2304,1024]{1,0:T(8,128)S(1)} %constant_dynamic-update-slice_fusion, f32[32,8,18,128]{3,2,1,0:T(8,128)S(1)} %bitcast.25), kind=kOutput, calls=%fused_computation | convolution fusion | flops 7247757312 | bytes 12845056 | tf_op jit(solution)/shard_map/dot_general | solution.py:53
  144.5 32.7 %all_to_all.30 = f32[8,32,1024]{2,1,0:T(8,128)S(1)} all-to-all(f32[8,32,1024]{2,1,0:T(8,128)S(1)} %bitcast.27), channel_id=1, replica_groups=mesh['row'=32,'col'=8] {'col'}, dimensions={0} | all-to-all | bytes 2097152 | tf_op jit(solution)/shard_map/all_to_all | solution.py:60
  177.4 48.4 %all_to_all.31 = f32[32,32,256]{2,1,0:T(8,128)} all-to-all(f32[32,32,256]{2,1,0:T(8,128)S(1)} %bitcast.30), channel_id=1, replica_groups=mesh['row'=32,'col'=8] {'row'}, dimensions={0} | all-to-all | bytes 2097152 | tf_op jit(solution)/shard_map/all_to_all | solution.py:66
  225.8 6.1 %all-to-all-start.2 = ((f32[8,4,32,256]{3,2,1,0:T(8,128)}), f32[8,4,32,256]{3,2,1,0:T(8,128)}, u32[]{:S(2)}, u32[]{:S(2)}) async-start(f32[8,4,32,256]{3,2,1,0:T(8,128)} %bitcast.29), calls=%async_computation.2 | async-start | bytes 2097152 | tf_op jit(solution)/shard_map/all_to_all | solution.py:68
  232.0 25.3 %all-to-all-done.2 = f32[8,4,32,256]{3,2,1,0:T(8,128)} async-done(((f32[8,4,32,256]{3,2,1,0:T(8,128)}), f32[8,4,32,256]{3,2,1,0:T(8,128)}, u32[]{:S(2)}, u32[]{:S(2)}) %all-to-all-start.2) | async-done | bytes 1048608 | tf_op jit(solution)/shard_map/all_to_all | solution.py:68
  263.9 5.2 collective-permute-start.8
  271.6 3.5 collective-permute-start.10
  275.2 3.1 collective-permute-start.11
  280.5 12.1 %collective-permute-done.8 = f32[256,1024]{1,0:T(8,128)S(1)} collective-permute-done((f32[256,1024]{1,0:T(8,128)S(1)}, f32[256,1024]{1,0:T(8,128)S(1)}, u32[]{:S(2)}, u32[]{:S(2)}) %collective-permute-start.8) | collective-permute-done | bytes 1048608 | tf_op jit(solution)/shard_map/ppermute | solution.py:16
  292.5 4.7 collective-permute-start.13
  297.3 16.4 %collective-permute-done.9 = f32[256,1024]{1,0:T(8,128)S(1)} collective-permute-done((f32[256,1024]{1,0:T(8,128)S(1)}, f32[256,1024]{1,0:T(8,128)S(1)}, u32[]{:S(2)}, u32[]{:S(2)}) %collective-permute-start.9) | collective-permute-done | bytes 1048608 | tf_op jit(solution)/shard_map/ppermute | solution.py:16
  313.7 6.1 %collective-permute-start.14 = (f32[256,1024]{1,0:T(8,128)S(1)}, f32[256,1024]{1,0:T(8,128)S(1)}, u32[]{:S(2)}, u32[]{:S(2)}) collective-permute-start(f32[256,1024]{1,0:T(8,128)S(1)} %multiply_add_fusion), channel_id=1, source_target_pairs={{24,0},{32,8},{40,16},{48,24},{56,32},{64,40},{72,48},{80,56},{88,... | collective-permute-start | bytes 3145736 | tf_op jit(solution)/shard_map/ppermute | solution.py:16
  319.8 21.9 %collective-permute-done.10 = f32[256,1024]{1,0:T(8,128)S(1)} collective-permute-done((f32[256,1024]{1,0:T(8,128)S(1)}, f32[256,1024]{1,0:T(8,128)S(1)}, u32[]{:S(2)}, u32[]{:S(2)}) %collective-permute-start.10) | collective-permute-done | bytes 1048608 | tf_op jit(solution)/shard_map/ppermute | solution.py:16
  344.0 20.2 %collective-permute-done.12 = f32[256,1024]{1,0:T(8,128)S(1)} collective-permute-done((f32[256,1024]{1,0:T(8,128)S(1)}, f32[256,1024]{1,0:T(8,128)S(1)}, u32[]{:S(2)}, u32[]{:S(2)}) %collective-permute-start.12) | collective-permute-done | bytes 1048608 | tf_op jit(solution)/shard_map/ppermute | solution.py:16
  364.4 24.4 %collective-permute-done.14 = f32[256,1024]{1,0:T(8,128)S(1)} collective-permute-done((f32[256,1024]{1,0:T(8,128)S(1)}, f32[256,1024]{1,0:T(8,128)S(1)}, u32[]{:S(2)}, u32[]{:S(2)}) %collective-permute-start.14) | collective-permute-done | bytes 1048608 | tf_op jit(solution)/shard_map/ppermute | solution.py:16
  388.9 12.0 %collective-permute-done.15 = f32[256,1024]{1,0:T(8,128)S(1)} collective-permute-done((f32[256,1024]{1,0:T(8,128)S(1)}, f32[256,1024]{1,0:T(8,128)S(1)}, u32[]{:S(2)}, u32[]{:S(2)}) %collective-permute-start.15) | collective-permute-done | bytes 1048608 | tf_op jit(solution)/shard_map/ppermute | solution.py:16
  401.0 8.3 %fusion.2 = f32[256,1024]{1,0:T(8,128)S(1)} fusion(f32[2304,1024]{1,0:T(8,128)S(1)} %constant_dynamic-update-slice_fusion.9, f32[32,8,18,128]{3,2,1,0:T(8,128)S(1)} %bitcast.26), kind=kOutput, calls=%fused_computation.2 | convolution fusion | flops 7247757312 | bytes 12845056 | tf_op jit(solution)/shard_map/dot_general | solution.py:53
  410.2 30.3 %all_to_all.32 = f32[8,32,1024]{2,1,0:T(8,128)S(1)} all-to-all(f32[8,32,1024]{2,1,0:T(8,128)S(1)} %bitcast.28), channel_id=1, replica_groups=mesh['row'=32,'col'=8] {'col'}, dimensions={0} | all-to-all | bytes 2097152 | tf_op jit(solution)/shard_map/all_to_all | solution.py:60
  440.7 46.5 %all_to_all.33 = f32[32,32,256]{2,1,0:T(8,128)S(1)} all-to-all(f32[32,32,256]{2,1,0:T(8,128)S(1)} %bitcast.31), channel_id=1, replica_groups=mesh['row'=32,'col'=8] {'row'}, dimensions={0} | all-to-all | bytes 2097152 | tf_op jit(solution)/shard_map/all_to_all | solution.py:66
  487.2 32.5 %all_to_all.34 = f32[8,4,32,256]{3,2,1,0:T(8,128)S(1)} all-to-all(f32[8,4,32,256]{3,2,1,0:T(8,128)S(1)} %bitcast.33), channel_id=1, replica_groups=mesh['row'=32,'col'=8] {'col'}, dimensions={0} | all-to-all | bytes 2097152 | tf_op jit(solution)/shard_map/all_to_all | solution.py:68
  523.4 3.5 fusion.10
  (53 shorter events, 36.6 us)
Async XLA Ops:
  0.0 54.3 %copy-start = (f32[2,16,128,128]{3,2,1,0:T(8,128)S(1)}, f32[2,16,128,128]{3,2,1,0:T(8,128)}, u32[]{:S(2)}) copy-start(f32[2,16,128,128]{3,2,1,0:T(8,128)} %param.5) | copy-start | bytes 6291460
  0.0 86.0 %copy-start.3 = (f32[256,1024]{1,0:T(8,128)S(1)}, f32[256,1024]{1,0:T(8,128)}, u32[]{:S(2)}) copy-start(f32[256,1024]{1,0:T(8,128)} %param.4) | copy-start | bytes 3145732
  0.0 27.4 %collective-permute-start = (f32[256,1024]{1,0:T(8,128)}, f32[256,1024]{1,0:T(8,128)}, u32[]{:S(2)}, u32[]{:S(2)}) collective-permute-start(f32[256,1024]{1,0:T(8,128)} %param.4), channel_id=1, source_target_pairs={{0,32},{8,40},{16,48},{24,56},{32,64},{40,72},{48,80},{56,88},{64,... | collective-permute-start | bytes 3145736 | tf_op jit(solution)/shard_map/ppermute | solution.py:16
  3.8 47.0 %collective-permute-start.1 = (f32[256,1024]{1,0:T(8,128)}, f32[256,1024]{1,0:T(8,128)}, u32[]{:S(2)}, u32[]{:S(2)}) collective-permute-start(f32[256,1024]{1,0:T(8,128)} %param.4), channel_id=1, source_target_pairs={{0,24},{8,32},{16,40},{24,48},{32,56},{40,64},{48,72},{56,80},{64,... | collective-permute-start | bytes 3145736 | tf_op jit(solution)/shard_map/ppermute | solution.py:16
  5.7 70.7 %collective-permute-start.2 = (f32[256,1024]{1,0:T(8,128)}, f32[256,1024]{1,0:T(8,128)}, u32[]{:S(2)}, u32[]{:S(2)}) collective-permute-start(f32[256,1024]{1,0:T(8,128)} %param.4), channel_id=1, source_target_pairs={{0,16},{8,24},{16,32},{24,40},{32,48},{40,56},{48,64},{56,72},{64,... | collective-permute-start | bytes 3145736 | tf_op jit(solution)/shard_map/ppermute | solution.py:16
  9.5 75.1 %collective-permute-start.3 = (f32[256,1024]{1,0:T(8,128)}, f32[256,1024]{1,0:T(8,128)}, u32[]{:S(2)}, u32[]{:S(2)}) collective-permute-start(f32[256,1024]{1,0:T(8,128)} %param.4), channel_id=1, source_target_pairs={{0,8},{8,16},{16,24},{24,32},{32,40},{40,48},{48,56},{56,64},{64,7... | collective-permute-start | bytes 3145736 | tf_op jit(solution)/shard_map/ppermute | solution.py:16
  12.6 86.3 %collective-permute-start.4 = (f32[256,1024]{1,0:T(8,128)}, f32[256,1024]{1,0:T(8,128)}, u32[]{:S(2)}, u32[]{:S(2)}) collective-permute-start(f32[256,1024]{1,0:T(8,128)} %param.4), channel_id=1, source_target_pairs={{8,0},{16,8},{24,16},{32,24},{40,32},{48,40},{56,48},{64,56},{72,6... | collective-permute-start | bytes 3145736 | tf_op jit(solution)/shard_map/ppermute | solution.py:16
  27.4 72.8 %collective-permute-start.5 = (f32[256,1024]{1,0:T(8,128)}, f32[256,1024]{1,0:T(8,128)S(1)}, u32[]{:S(2)}, u32[]{:S(2)}) collective-permute-start(f32[256,1024]{1,0:T(8,128)} %param.4), channel_id=1, source_target_pairs={{16,0},{24,8},{32,16},{40,24},{48,32},{56,40},{64,48},{72,56},{80,... | collective-permute-start | bytes 3145736 | tf_op jit(solution)/shard_map/ppermute | solution.py:16
  50.9 70.4 %collective-permute-start.6 = (f32[256,1024]{1,0:T(8,128)}, f32[256,1024]{1,0:T(8,128)S(1)}, u32[]{:S(2)}, u32[]{:S(2)}) collective-permute-start(f32[256,1024]{1,0:T(8,128)} %param.4), channel_id=1, source_target_pairs={{24,0},{32,8},{40,16},{48,24},{56,32},{64,40},{72,48},{80,56},{88,... | collective-permute-start | bytes 3145736 | tf_op jit(solution)/shard_map/ppermute | solution.py:16
  57.0 79.2 %copy-start.1 = (f32[2,18,128,128]{3,1,2,0:T(8,128)}, f32[2,18,128,128]{3,1,2,0:T(8,128)S(1)}, u32[]{:S(2)}) copy-start(f32[2,18,128,128]{3,1,2,0:T(8,128)S(1)} %fusion.4) | copy-start | bytes 7077892
  76.4 59.8 %collective-permute-start.7 = (f32[256,1024]{1,0:T(8,128)}, f32[256,1024]{1,0:T(8,128)S(1)}, u32[]{:S(2)}, u32[]{:S(2)}) collective-permute-start(f32[256,1024]{1,0:T(8,128)} %param.4), channel_id=1, source_target_pairs={{32,0},{40,8},{48,16},{56,24},{64,32},{72,40},{80,48},{88,56},{96,... | collective-permute-start | bytes 3145736 | tf_op jit(solution)/shard_map/ppermute | solution.py:16
  144.5 117.6 %copy-start.5 = (f32[256]{0:T(256)S(1)}, f32[256]{0:T(256)}, u32[]{:S(2)}) copy-start(f32[256]{0:T(256)} %param.7) | copy-start | bytes 3076
  225.8 31.4 %all-to-all-start.2 = ((f32[8,4,32,256]{3,2,1,0:T(8,128)}), f32[8,4,32,256]{3,2,1,0:T(8,128)}, u32[]{:S(2)}, u32[]{:S(2)}) async-start(f32[8,4,32,256]{3,2,1,0:T(8,128)} %bitcast.29), calls=%async_computation.2 | async-start | bytes 2097152 | tf_op jit(solution)/shard_map/all_to_all | solution.py:68
  263.9 137.1 %copy-start.2 = (f32[2,18,128,128]{3,1,2,0:T(8,128)S(1)}, f32[2,18,128,128]{3,1,2,0:T(8,128)}, u32[]{:S(2)}) copy-start(f32[2,18,128,128]{3,1,2,0:T(8,128)} %copy-done.1) | copy-start | bytes 7077892
  263.9 28.7 %collective-permute-start.8 = (f32[256,1024]{1,0:T(8,128)S(1)}, f32[256,1024]{1,0:T(8,128)S(1)}, u32[]{:S(2)}, u32[]{:S(2)}) collective-permute-start(f32[256,1024]{1,0:T(8,128)S(1)} %multiply_add_fusion), channel_id=1, source_target_pairs={{0,32},{8,40},{16,48},{24,56},{32,64},{40,72},{48,80},{56,88},{64,... | collective-permute-start | bytes 3145736 | tf_op jit(solution)/shard_map/ppermute | solution.py:16
  269.1 44.6 %collective-permute-start.9 = (f32[256,1024]{1,0:T(8,128)S(1)}, f32[256,1024]{1,0:T(8,128)S(1)}, u32[]{:S(2)}, u32[]{:S(2)}) collective-permute-start(f32[256,1024]{1,0:T(8,128)S(1)} %multiply_add_fusion), channel_id=1, source_target_pairs={{0,24},{8,32},{16,40},{24,48},{32,56},{40,64},{48,72},{56,80},{64,... | collective-permute-start | bytes 3145736 | tf_op jit(solution)/shard_map/ppermute | solution.py:16
  271.6 70.1 %collective-permute-start.10 = (f32[256,1024]{1,0:T(8,128)S(1)}, f32[256,1024]{1,0:T(8,128)S(1)}, u32[]{:S(2)}, u32[]{:S(2)}) collective-permute-start(f32[256,1024]{1,0:T(8,128)S(1)} %multiply_add_fusion), channel_id=1, source_target_pairs={{0,16},{8,24},{16,32},{24,40},{32,48},{40,56},{48,64},{56,72},{64,... | collective-permute-start | bytes 3145736 | tf_op jit(solution)/shard_map/ppermute | solution.py:16
  275.2 68.7 %collective-permute-start.11 = (f32[256,1024]{1,0:T(8,128)S(1)}, f32[256,1024]{1,0:T(8,128)S(1)}, u32[]{:S(2)}, u32[]{:S(2)}) collective-permute-start(f32[256,1024]{1,0:T(8,128)S(1)} %multiply_add_fusion), channel_id=1, source_target_pairs={{0,8},{8,16},{16,24},{24,32},{32,40},{40,48},{48,56},{56,64},{64,7... | collective-permute-start | bytes 3145736 | tf_op jit(solution)/shard_map/ppermute | solution.py:16
  278.3 85.9 %collective-permute-start.12 = (f32[256,1024]{1,0:T(8,128)S(1)}, f32[256,1024]{1,0:T(8,128)S(1)}, u32[]{:S(2)}, u32[]{:S(2)}) collective-permute-start(f32[256,1024]{1,0:T(8,128)S(1)} %multiply_add_fusion), channel_id=1, source_target_pairs={{8,0},{16,8},{24,16},{32,24},{40,32},{48,40},{56,48},{64,56},{72,6... | collective-permute-start | bytes 3145736 | tf_op jit(solution)/shard_map/ppermute | solution.py:16
  292.5 71.7 %collective-permute-start.13 = (f32[256,1024]{1,0:T(8,128)S(1)}, f32[256,1024]{1,0:T(8,128)S(1)}, u32[]{:S(2)}, u32[]{:S(2)}) collective-permute-start(f32[256,1024]{1,0:T(8,128)S(1)} %multiply_add_fusion), channel_id=1, source_target_pairs={{16,0},{24,8},{32,16},{40,24},{48,32},{56,40},{64,48},{72,56},{80,... | collective-permute-start | bytes 3145736 | tf_op jit(solution)/shard_map/ppermute | solution.py:16
  313.7 75.1 %collective-permute-start.14 = (f32[256,1024]{1,0:T(8,128)S(1)}, f32[256,1024]{1,0:T(8,128)S(1)}, u32[]{:S(2)}, u32[]{:S(2)}) collective-permute-start(f32[256,1024]{1,0:T(8,128)S(1)} %multiply_add_fusion), channel_id=1, source_target_pairs={{24,0},{32,8},{40,16},{48,24},{56,32},{64,40},{72,48},{80,56},{88,... | collective-permute-start | bytes 3145736 | tf_op jit(solution)/shard_map/ppermute | solution.py:16
  341.7 59.2 %collective-permute-start.15 = (f32[256,1024]{1,0:T(8,128)S(1)}, f32[256,1024]{1,0:T(8,128)S(1)}, u32[]{:S(2)}, u32[]{:S(2)}) collective-permute-start(f32[256,1024]{1,0:T(8,128)S(1)} %multiply_add_fusion), channel_id=1, source_target_pairs={{32,0},{40,8},{48,16},{56,24},{64,32},{72,40},{80,48},{88,56},{96,... | collective-permute-start | bytes 3145736 | tf_op jit(solution)/shard_map/ppermute | solution.py:16
  409.3 1.0 copy-start.4
where the time goes:
time: 531 us; the launch traced here: 527 us
  waiting for transfers between devices  231 us (44%)
  blocking collectives  190 us (36%)
  starting transfers between devices  62.3 us (12%)
  matrix products  19.2 us (4%)
  local copies, waits for them, and re-layouts  17.4 us (3%)
  other arithmetic  6.14 us (1%)
    ppermute x16, waiting for transfers between devices, shifted(): return lax.ppermute(array, axis, pairs)  206 us
    all_to_all x3, blocking collectives, mirrored(): lax.all_to_all(moved, 'col', split_axis=0, concat_axis=0, tiled=True)  95.5 us
    all_to_all x2, blocking collectives, mirrored(): lax.all_to_all(moved, 'row', split_axis=0, concat_axis=0, tiled=True)  95 us
    ppermute x16, starting transfers between devices, shifted(): return lax.ppermute(array, axis, pairs)  56.2 us
    all_to_all x1, waiting for transfers between devices, mirrored(): lax.all_to_all(moved, 'col', split_axis=0, concat_axis=0, tiled=True)  25.3 us
    dot_general x2, matrix products, forward(): jnp.dot(row_band, extended, precision=lax.Precision.HIGHEST, preferred_el...  16.5 us
  transfers between devices with their start and end apart: 17, of which 13 were waited for; matrix products, arithmetic and copies ran while one was open for 2% of the time, Pallas kernels for 0%

commit v1 on v0

v1 whole, which is shorter than its diff:
```python
import jax
import jax.numpy as jnp
from jax import lax
from jax.experimental import pallas as pl
from jax.experimental.pallas import tpu as pltpu
from jax.sharding import PartitionSpec as P

BS = 128
REACH = 8
WIDTH = 2 * REACH + 1
HALF = 256
TILE = 512
SPAN = (WIDTH + 1) * BS
MESH = pl.DeviceIdType.MESH
F32 = jnp.float32
BF16 = jnp.bfloat16

S_RELAYOUT, S_NOISE, S_BAND, S_FWD, S_HALO, S_MIRROR, S_BACK, N_SEND = 0, 4, 6, 10, 11, 27, 31, 35
R_RELAYOUT, R_NOISE, R_BAND, R_HALO, R_MIRROR, R_BACK, N_RECV = 0, 4, 6, 10, 26, 30, 34


def kernel(
    slot_ref, p_ref, a_ref, q_ref, o_ref,
    band, band_hi, band_lo, ext_p, ext_k, ext_hi, ext_lo,
    first, first_t, total, total_t, result, noise, send, recv,
):
    row = lax.axis_index("row")
    col = lax.axis_index("col")
    x, z0, y = row % 4, (row // 4) % 2, row // 8
    core, zh = col % 2, col // 2
    tile_i, tile_j = 4 * y + 2 * z0 + core, 4 * zh + x

    def device(x, y, z0, zh, core):
        return (8 * y + 4 * z0 + x, 2 * zh + core)

    def remote(src, dst, target, s, r):
        return pltpu.make_async_remote_copy(
            src_ref=src, dst_ref=dst, send_sem=send.at[s], recv_sem=recv.at[r],
            device_id=target, device_id_type=MESH,
        )

    pending = []

    def start(src, dst, target, s, r, local=None):
        copy = remote(src, dst, target, s, r)
        if local is None:
            copy.start()
            pending.append((None, copy))
            return
        pl.when(jnp.logical_not(local))(copy.start)
        pl.when(local)(pltpu.make_async_copy(src, dst, recv.at[r]).start)
        pending.append((jnp.logical_not(local), copy))

    def arrived(dst, r):
        remote(dst, dst, (row, col), 0, r).wait_recv()

    partner = device(x, y, z0, zh, 1 - core)

    mine = x // 2 == core
    part = x % 2
    for h in range(2):
        target = device(2 * core + h, y, z0, zh, x // 2)
        local = jnp.logical_and(mine, part == h)
        start(q_ref, noise.at[part], target, S_NOISE + h, R_NOISE + part, local)
    for cc in range(2):
        for h in range(2):
            target = device(2 * core + h, y, z0, zh, x // 2)
            local = jnp.logical_and(mine, part == h)
            start(
                p_ref.at[:, pl.ds(TILE * h + HALF * cc, HALF)],
                ext_p.at[cc, pl.ds(pl.multiple_of(2 * TILE + HALF * part, HALF), HALF), :],
                target, S_RELAYOUT + 2 * cc + h, R_RELAYOUT + 2 * cc + part, local,
            )

    def right(x):
        return (x + 1) % 4

    def left(x):
        return (x + 3) % 4

    @pl.when(mine)
    def _():
        for b in range(2):
            for d in range(WIDTH):
                slot = slot_ref[b, d]
                block = a_ref[b, jnp.maximum(slot, 0)]
                band[part, b, :, d * BS:(d + 1) * BS] = jnp.where(slot >= 0, block, 0.0)
        for t, b in enumerate((0, 1)):
            remote(band.at[part, b], band.at[part, b], device(right(x), y, z0, zh, core),
                   S_BAND + t, R_BAND + 2 * part + b).start()
            remote(band.at[part, 1 - b], band.at[part, 1 - b], device(left(x), y, z0, zh, core),
                   S_BAND + 2 + t, R_BAND + 2 * part + 1 - b).start()

    step = (x + 4 - 2 * core) % 4
    fwd_c = 1 - step % 2
    fwd_right = jnp.logical_or(step == 1, step == 2)
    fwd_b = jnp.where(fwd_right, 0, 1)
    fwd_x = jnp.where(fwd_right, right(x), left(x))

    def forward_band():
        unit = band.at[fwd_c, fwd_b]
        arrived(unit, R_BAND + 2 * fwd_c + fwd_b)
        start(unit, unit, device(fwd_x, y, z0, zh, core), S_FWD, R_BAND + 2 * fwd_c + fwd_b)

    d_slot = jnp.where(z0 == 0, 4, 0)
    y_slot = 4 - d_slot
    y_next = jnp.where(z0 == 0, (y + 1) % 4, (y + 3) % 4)
    near = jnp.where(core == 0, 1, 3)
    f_slot = jnp.where(core == 0, 4, 0)
    f_dst = jnp.where(core == 0, 3, 1)
    f_from_z = f_slot == d_slot

    def halo(ext, base):
        def at(cc, slot):
            return ext.at[cc, pl.ds(pl.multiple_of(slot * TILE, TILE), TILE), :]

        def sem(kind, cc):
            return 8 * base + 2 * kind + cc

        def own(cc):
            start(at(cc, 2), at(cc, y_slot), device(x, y, 1 - z0, zh, core),
                  S_HALO + sem(0, cc), R_HALO + sem(0, cc))
            start(at(cc, 2), at(cc, near), partner, S_HALO + sem(1, cc), R_HALO + sem(1, cc))

        def across(cc):
            start(at(cc, f_slot), at(cc, f_dst), partner,
                  S_HALO + sem(3, cc), R_HALO + sem(3, cc))

        def from_z(cc):
            arrived(at(cc, d_slot), R_HALO + sem(0, cc))
            start(at(cc, d_slot), at(cc, y_slot), device(x, y_next, z0, zh, core),
                  S_HALO + sem(2, cc), R_HALO + sem(2, cc))
            pl.when(f_from_z)(lambda: remote(
                at(cc, f_slot), at(cc, f_dst), partner,
                S_HALO + sem(3, cc), R_HALO + sem(3, cc)).start())

        def from_y(cc):
            arrived(at(cc, y_slot), R_HALO + sem(2, cc))
            pl.when(jnp.logical_not(f_from_z))(lambda: remote(
                at(cc, f_slot), at(cc, f_dst), partner,
                S_HALO + sem(3, cc), R_HALO + sem(3, cc)).start())
            pending.append((None, remote(
                at(cc, f_slot), at(cc, f_dst), partner,
                S_HALO + sem(3, cc), R_HALO + sem(3, cc))))

        def rest(cc):
            arrived(at(cc, 4 - near), R_HALO + sem(1, cc))
            arrived(at(cc, 4 - f_dst), R_HALO + sem(3, cc))

        return own, from_z, from_y, rest

    def split(ext, cc):
        def piece(n, _):
            rows = pl.ds(pl.multiple_of(n * BS, BS), BS)
            value = ext[cc, rows, :]
            hi = value.astype(BF16)
            ext_hi[cc, rows, :] = hi
            ext_lo[cc, rows, :] = (value - hi.astype(F32)).astype(BF16)
            return 0
        lax.fori_loop(0, 5 * TILE // BS, piece, 0)

    def product(c, cc):
        rows = slice(HALF * c, HALF * c + SPAN)
        hi, lo = ext_hi[cc, rows, :], ext_lo[cc, rows, :]
        acc = jnp.dot(band_hi[c], hi, preferred_element_type=F32)
        acc += jnp.dot(band_hi[c], lo, preferred_element_type=F32)
        acc += jnp.dot(band_lo[c], hi, preferred_element_type=F32)
        return acc

    def split_band(c):
        for b in range(2):
            empty = slice(0, BS) if b else slice(WIDTH * BS, SPAN)
            rows = slice(b * BS, (b + 1) * BS)
            band_hi[c, rows, empty] = jnp.zeros((BS, BS), BF16)
            band_lo[c, rows, empty] = jnp.zeros((BS, BS), BF16)
            for d in range(WIDTH):
                value = band[c, b, :, d * BS:(d + 1) * BS]
                hi = value.astype(BF16)
                cols = slice((b + d) * BS, (b + d + 1) * BS)
                band_hi[c, rows, cols] = hi
                band_lo[c, rows, cols] = (value - hi.astype(F32)).astype(BF16)

    mirror = device(2 * z0 + core, zh, x // 2, y, x % 2)
    on_diagonal = tile_i == tile_j
    eye = (
        lax.broadcasted_iota(jnp.int32, (HALF, HALF), 0)
        == lax.broadcasted_iota(jnp.int32, (HALF, HALF), 1)
    )

    def diagonal(c):
        values = jnp.broadcast_to(noise[c, 0:1, :], (HALF, HALF))
        return jnp.where(jnp.logical_and(eye, on_diagonal), values, 0.0)

    own, from_z, from_y, rest = halo(ext_p, 0)
    for cc in range(2):
        for c in range(2):
            arrived(ext_p.at[cc, pl.ds(2 * TILE + HALF * c, HALF), :], R_RELAYOUT + 2 * cc + c)
        own(cc)
    from_z(0)
    from_z(1)
    from_y(0)
    from_y(1)
    forward_band()
    for cc in range(2):
        rest(cc)
        split(ext_p, cc)
    for c in range(2):
        arrived(noise.at[c], R_NOISE + c)

    for c in range(2):
        for b in range(2):
            seen = jnp.logical_and(fwd_c == c, fwd_b == b)
            held = jnp.logical_and(mine, part == c)
            skip = jnp.logical_or(seen, held)
            pl.when(jnp.logical_not(skip))(
                lambda c=c, b=b: arrived(band.at[c, b], R_BAND + 2 * c + b))
        split_band(c)
        for cc in range(2):
            first[c, cc] = product(c, cc)
        start(first.at[c], first_t.at[c], mirror, S_MIRROR + c, R_MIRROR + c, on_diagonal)

    own, from_z, from_y, rest = halo(ext_k, 1)
    for cc in range(2):
        arrived(first_t.at[cc], R_MIRROR + cc)
        for c in range(2):
            k = first[c, cc] + first_t[cc, c].T
            if c == cc:
                k += diagonal(c)
            ext_k[cc, 2 * TILE + HALF * c:2 * TILE + HALF * (c + 1), :] = k
        own(cc)
    from_z(0)
    from_z(1)
    from_y(0)
    for cc in range(2):
        if cc:
            from_y(1)
        rest(cc)
        split(ext_k, cc)
        for c in range(2):
            total[cc, c] = 0.25 * first[c, cc] + 0.03125 * product(c, cc)
        start(total.at[cc], total_t.at[cc], mirror, S_MIRROR + 2 + cc, R_MIRROR + 2 + cc, on_diagonal)

    for c in range(2):
        arrived(total_t.at[c], R_MIRROR + 2 + c)
        target = device(2 * core + c, y, z0, zh, x // 2)
        local = jnp.logical_and(mine, part == c)
        for cc in range(2):
            p = ext_p[cc, 2 * TILE + HALF * c:2 * TILE + HALF * (c + 1), :]
            value = p + (total[cc, c] + total_t[c, cc].T)
            if c == cc:
                value += 0.25 * diagonal(c)
            result[c, cc] = value
            start(
                result.at[c, cc],
                o_ref.at[:, pl.ds(pl.multiple_of(TILE * part + HALF * cc, HALF), HALF)],
                target, S_BACK + 2 * c + cc, R_BACK + 2 * part + cc, local,
            )
    for h in range(2):
        for cc in range(2):
            arrived(o_ref.at[:, pl.ds(TILE * h + HALF * cc, HALF)], R_BACK + 2 * h + cc)

    @pl.when(mine)
    def _():
        for t in range(4):
            remote(band.at[0, 0], band.at[0, 0], (row, col), S_BAND + t, 0).wait_send()

    for condition, copy in pending:
        if condition is None:
            copy.wait_send()
        else:
            pl.when(condition)(copy.wait_send)


def body(p_cov, a_blocks, pattern, q_diag):
    base = lax.axis_index("row") * 2
    wanted = (
        base
        + jnp.arange(2, dtype=jnp.int32)[:, None]
        + jnp.arange(WIDTH, dtype=jnp.int32)[None, :]
        - REACH
    )
    hit = pattern[:, None, :] == wanted[:, :, None]
    slots = jnp.max(
        jnp.where(hit, jnp.arange(pattern.shape[1], dtype=jnp.int32)[None, None, :], -1), axis=2
    )
    slots = jnp.where(jnp.logical_and(wanted >= 0, wanted < 64), slots, -1)
    noise = jnp.broadcast_to(q_diag[None, :], (8, HALF))
    vmem = pl.BlockSpec(memory_space=pltpu.VMEM)
    return pl.pallas_call(
        kernel,
        out_shape=jax.ShapeDtypeStruct(p_cov.shape, F32),
        in_specs=[pl.BlockSpec(memory_space=pltpu.SMEM), vmem, vmem, vmem],
        out_specs=vmem,
        scratch_shapes=[
            pltpu.VMEM((2, 2, BS, WIDTH * BS), F32),
            pltpu.VMEM((2, HALF, SPAN), BF16),
            pltpu.VMEM((2, HALF, SPAN), BF16),
            pltpu.VMEM((2, 5 * TILE, HALF), F32),
            pltpu.VMEM((2, 5 * TILE, HALF), F32),
            pltpu.VMEM((2, 5 * TILE, HALF), BF16),
            pltpu.VMEM((2, 5 * TILE, HALF), BF16),
            pltpu.VMEM((2, 2, HALF, HALF), F32),
            pltpu.VMEM((2, 2, HALF, HALF), F32),
            pltpu.VMEM((2, 2, HALF, HALF), F32),
            pltpu.VMEM((2, 2, HALF, HALF), F32),
            pltpu.VMEM((2, 2, HALF, HALF), F32),
            pltpu.VMEM((2, 8, HALF), F32),
            pltpu.SemaphoreType.DMA((N_SEND,)),
            pltpu.SemaphoreType.DMA((N_RECV,)),
        ],
        compiler_params=pltpu.CompilerParams(has_side_effects=True, vmem_limit_bytes=60 * 1024 * 1024),
    )(slots, p_cov, a_blocks, noise)


def solution(mesh):
    return jax.shard_map(
        body,
        mesh=mesh,
        in_specs=(P("row", "col"), P("row", None, None, None), P("row", None), P("row")),
        out_specs=P("row", "col"),
        check_vma=False,
    )
```

time: 531 us -> 348 us (0.66)
  the two profiles are of different devices: /device:TPU:27 before, /device:TPU:211 now
where the time goes in v1:
time: 348 us; the launch traced here: 347 us
  Pallas kernels  342 us (98%)
  local copies, waits for them, and re-layouts  3.58 us (1%)
    pallas_call x1, Pallas kernels, body(): pl.pallas_call(kernel, out_shape=jax.ShapeDtypeStruct(p_cov.shape, F32),...  342 us

profile of v1, /device:TPU:211, one launch (start us, length us, event | category | flops | bytes accessed | tf_op | source)
XLA Modules:
  0.0 347.5 jit_solution(5019747588604553492)
XLA Ops:
  0.0 0.1 add_add_fusion
  0.1 0.8 select_reduce_fusion
  0.8 0.7 and_select_fusion.slot_ref
  1.5 1.3 broadcast_in_dim.30.q_ref
  2.8 342.4 %shard_map.46 = f32[256,1024]{1,0:T(8,128)} custom-call(s32[2,17]{1,0:T(2,128)} %and_select_fusion.slot_ref, f32[256,1024]{1,0:T(8,128)} %p_ref.1, f32[2,16,128,128]{3,2,1,0:T(8,128)} %a_ref.1, f32[8,256]{1,0:T(8,128)} %broadcast_in_dim.30.q_ref), custom_call_target="tpu_custom_call" | custom-call | tf_op jit(solution)/shard_map/pallas_call | solution.py:289
  345.2 2.3 copy.6
  (1 shorter events, 0.0 us)

commit v2 on v1

--- a/solution.py
+++ b/solution.py
@@ -9,20 +9,21 @@
 REACH = 8
 WIDTH = 2 * REACH + 1
 HALF = 256
+QUARTER = 64
 TILE = 512
 SPAN = (WIDTH + 1) * BS
 MESH = pl.DeviceIdType.MESH
 F32 = jnp.float32
 BF16 = jnp.bfloat16
 
-S_RELAYOUT, S_NOISE, S_BAND, S_FWD, S_HALO, S_MIRROR, S_BACK, N_SEND = 0, 4, 6, 10, 11, 27, 31, 35
-R_RELAYOUT, R_NOISE, R_BAND, R_HALO, R_MIRROR, R_BACK, N_RECV = 0, 4, 6, 10, 26, 30, 34
+S_RELAYOUT, S_NOISE, S_BAND, S_FWD, S_HALO, S_MIRROR, S_BACK, N_SEND = 0, 4, 6, 8, 9, 25, 57, 61
+R_RELAYOUT, R_NOISE, R_BAND, R_HALO, R_MIRROR, R_BACK, N_RECV = 0, 4, 6, 10, 26, 58, 62
 
 
 def kernel(
     slot_ref, p_ref, a_ref, q_ref, o_ref,
-    band, band_hi, band_lo, ext_p, ext_k, ext_hi, ext_lo,
-    first, first_t, total, total_t, result, noise, send, recv,
+    strip, band, band_hi, band_lo, ext_p, ext_k, ext_hi, ext_lo,
+    first, first_m, first_t, total, total_m, total_t, result, noise, send, recv,
 ):
     row = lax.axis_index("row")
     col = lax.axis_index("col")
@@ -42,6 +43,9 @@
     pending = []
 
     def start(src, dst, target, s, r, local=None):
+        if local is True:
+            pltpu.make_async_copy(src, dst, recv.at[r]).start()
+            return
         copy = remote(src, dst, target, s, r)
         if local is None:
             copy.start()
@@ -78,18 +82,21 @@
     def left(x):
         return (x + 3) % 4
 
+    def block(b, d):
+        slot = slot_ref[b, d]
+        return jnp.where(slot >= 0, a_ref[b, jnp.maximum(slot, 0)], 0.0)
+
+    for d in range(WIDTH):
+        strip[:, d * BS:(d + 1) * BS] = block(core, d)
+    for t, near_x in enumerate((right(x), left(x))):
+        start(strip, band.at[part, core], device(near_x, y, z0, zh, x // 2),
+              S_BAND + t, R_BAND + 2 * part + core)
+
     @pl.when(mine)
     def _():
         for b in range(2):
             for d in range(WIDTH):
-                slot = slot_ref[b, d]
-                block = a_ref[b, jnp.maximum(slot, 0)]
-                band[part, b, :, d * BS:(d + 1) * BS] = jnp.where(slot >= 0, block, 0.0)
-        for t, b in enumerate((0, 1)):
-            remote(band.at[part, b], band.at[part, b], device(right(x), y, z0, zh, core),
-                   S_BAND + t, R_BAND + 2 * part + b).start()
-            remote(band.at[part, 1 - b], band.at[part, 1 - b], device(left(x), y, z0, zh, core),
-                   S_BAND + 2 + t, R_BAND + 2 * part + 1 - b).start()
+                band[part, b, :, d * BS:(d + 1) * BS] = block(b, d)
 
     step = (x + 4 - 2 * core) % 4
     fwd_c = 1 - step % 2
@@ -180,7 +187,33 @@
                 band_hi[c, rows, cols] = hi
                 band_lo[c, rows, cols] = (value - hi.astype(F32)).astype(BF16)
 
-    mirror = device(2 * z0 + core, zh, x // 2, y, x % 2)
+    def mirror(base, src, mid, dst):
+        def quarter(ref, c, n):
+            return ref.at[c, :, pl.ds(pl.multiple_of(n * QUARTER, QUARTER), QUARTER), :]
+
+        def spread(c):
+            for n in (1, 3, 2, 0):
+                r = (y + n) % 4
+                start(quarter(src, c, r), quarter(mid, c, y), device(x, r, z0, zh, core),
+                      S_MIRROR + 16 * base + 8 * c + n, R_MIRROR + 16 * base + 8 * c + y,
+                      None if n else True)
+
+        def onward(c):
+            for n in (0, 1, 3, 2):
+                r = (y + n) % 4
+                unit = quarter(mid, c, r)
+                arrived(unit, R_MIRROR + 16 * base + 8 * c + r)
+                here = (x == 2 * z0 + core) & (y == zh) & (z0 == x // 2) & (zh == r) & (core == x % 2)
+                start(unit, quarter(dst, c, y), device(2 * z0 + core, zh, x // 2, r, x % 2),
+                      S_MIRROR + 16 * base + 8 * c + 4 + n, R_MIRROR + 16 * base + 8 * c + 4 + y,
+                      here)
+
+        def landed(c):
+            for r in range(4):
+                arrived(quarter(dst, c, r), R_MIRROR + 16 * base + 8 * c + 4 + r)
+
+        return spread, onward, landed
+
     on_diagonal = tile_i == tile_j
     eye = (
         lax.broadcasted_iota(jnp.int32, (HALF, HALF), 0)
@@ -207,6 +240,7 @@
     for c in range(2):
         arrived(noise.at[c], R_NOISE + c)
 
+    spread, onward, landed = mirror(0, first, first_m, first_t)
     for c in range(2):
         for b in range(2):
             seen = jnp.logical_and(fwd_c == c, fwd_b == b)
@@ -217,11 +251,13 @@
         split_band(c)
         for cc in range(2):
             first[c, cc] = product(c, cc)
-        start(first.at[c], first_t.at[c], mirror, S_MIRROR + c, R_MIRROR + c, on_diagonal)
+        spread(c)
+    onward(0)
+    onward(1)
 
     own, from_z, from_y, rest = halo(ext_k, 1)
     for cc in range(2):
-        arrived(first_t.at[cc], R_MIRROR + cc)
+        landed(cc)
         for c in range(2):
             k = first[c, cc] + first_t[cc, c].T
             if c == cc:
@@ -231,17 +267,19 @@
     from_z(0)
     from_z(1)
     from_y(0)
-    for cc in range(2):
-        if cc:
-            from_y(1)
+    spread, onward, landed = mirror(1, total, total_m, total_t)
+    for cc in range(2):
         rest(cc)
         split(ext_k, cc)
         for c in range(2):
             total[cc, c] = 0.25 * first[c, cc] + 0.03125 * product(c, cc)
-        start(total.at[cc], total_t.at[cc], mirror, S_MIRROR + 2 + cc, R_MIRROR + 2 + cc, on_diagonal)
+        spread(cc)
+        if cc == 0:
+            from_y(1)
+        onward(cc)
 
     for c in range(2):
-        arrived(total_t.at[c], R_MIRROR + 2 + c)
+        landed(c)
         target = device(2 * core + c, y, z0, zh, x // 2)
         local = jnp.logical_and(mine, part == c)
         for cc in range(2):
@@ -258,11 +296,6 @@
     for h in range(2):
         for cc in range(2):
             arrived(o_ref.at[:, pl.ds(TILE * h + HALF * cc, HALF)], R_BACK + 2 * h + cc)
-
-    @pl.when(mine)
-    def _():
-        for t in range(4):
-            remote(band.at[0, 0], band.at[0, 0], (row, col), S_BAND + t, 0).wait_send()
 
     for condition, copy in pending:
         if condition is None:
@@ -292,6 +325,7 @@
         in_specs=[pl.BlockSpec(memory_space=pltpu.SMEM), vmem, vmem, vmem],
         out_specs=vmem,
         scratch_shapes=[
+            pltpu.VMEM((BS, WIDTH * BS), F32),
             pltpu.VMEM((2, 2, BS, WIDTH * BS), F32),
             pltpu.VMEM((2, HALF, SPAN), BF16),
             pltpu.VMEM((2, HALF, SPAN), BF16),
@@ -299,11 +333,7 @@
             pltpu.VMEM((2, 5 * TILE, HALF), F32),
             pltpu.VMEM((2, 5 * TILE, HALF), BF16),
             pltpu.VMEM((2, 5 * TILE, HALF), BF16),
-            pltpu.VMEM((2, 2, HALF, HALF), F32),
-            pltpu.VMEM((2, 2, HALF, HALF), F32),
-            pltpu.VMEM((2, 2, HALF, HALF), F32),
-            pltpu.VMEM((2, 2, HALF, HALF), F32),
-            pltpu.VMEM((2, 2, HALF, HALF), F32),
+            *[pltpu.VMEM((2, 2, HALF, HALF), F32)] * 7,
             pltpu.VMEM((2, 8, HALF), F32),
             pltpu.SemaphoreType.DMA((N_SEND,)),
             pltpu.SemaphoreType.DMA((N_RECV,)),

time: 348 us -> 201 us (0.58)
  the two profiles are of different devices: /device:TPU:211 before, /device:TPU:27 now
where the time goes in v2:
time: 201 us
  Pallas kernels  196 us (98%)
  local copies, waits for them, and re-layouts  3.58 us (2%)
    pallas_call x1, Pallas kernels, body(): pl.pallas_call(kernel, out_shape=jax.ShapeDtypeStruct(p_cov.shape, F32),...  196 us

profile of v2, /device:TPU:27, one launch (start us, length us, event | category | flops | bytes accessed | tf_op | source)
XLA Modules:
  0.0 201.2 jit_solution(11735087873368405458)
XLA Ops:
  0.0 0.1 add_add_fusion
  0.1 0.8 select_reduce_fusion
  0.8 0.7 and_select_fusion.slot_ref
  1.5 1.3 broadcast_in_dim.30.q_ref
  2.8 196.1 %shard_map.46 = f32[256,1024]{1,0:T(8,128)} custom-call(s32[2,17]{1,0:T(2,128)} %and_select_fusion.slot_ref, f32[256,1024]{1,0:T(8,128)} %p_ref.1, f32[2,16,128,128]{3,2,1,0:T(8,128)} %a_ref.1, f32[8,256]{1,0:T(8,128)} %broadcast_in_dim.30.q_ref), custom_call_target="tpu_custom_call" | custom-call | tf_op jit(solution)/shard_map/pallas_call | solution.py:322
  198.9 2.3 %copy.6 = f32[256,1024]{1,0:T(8,128)} copy(f32[256,1024]{1,0:T(8,128)} %shard_map.46) | data formatting | bytes 2097152
  (1 shorter events, 0.0 us)

commit v3 on v2

v3 whole, which is shorter than its diff:
```python
import jax
import jax.numpy as jnp
from jax import lax
from jax.experimental import pallas as pl
from jax.experimental.pallas import tpu as pltpu
from jax.sharding import PartitionSpec as P

BS = 128
REACH = 8
WIDTH = 2 * REACH + 1
HALF = 256
QUARTER = 64
TILE = 512
SPAN = (WIDTH + 1) * BS
MESH = pl.DeviceIdType.MESH
F32 = jnp.float32
BF16 = jnp.bfloat16

S_RELAYOUT, S_NOISE, S_BAND, S_FWD, S_HALO, S_MIRROR, S_BACK, N_SEND = 0, 4, 6, 8, 9, 41, 105, 109
R_RELAYOUT, R_NOISE, R_BAND, R_HALO, R_MIRROR, R_BACK, N_RECV = 0, 4, 6, 10, 42, 106, 110


def kernel(
    pattern_ref, p_ref, a_hbm, q_ref, o_ref,
    a_ref, own_noise, strip, band, band_hi, band_lo, ext_p, ext_k, ext_hi, ext_lo,
    first, first_m, first_t, total, total_m, total_t, result, noise, send, recv, load,
):
    row = lax.axis_index("row")
    col = lax.axis_index("col")
    x, z0, y = row % 4, (row // 4) % 2, row // 8
    core, zh = col % 2, col // 2
    tile_i, tile_j = 4 * y + 2 * z0 + core, 4 * zh + 2 * (x % 2) + x // 2

    def device(x, y, z0, zh, core):
        return (8 * y + 4 * z0 + x, 2 * zh + core)

    def remote(src, dst, target, s, r):
        return pltpu.make_async_remote_copy(
            src_ref=src, dst_ref=dst, send_sem=send.at[s], recv_sem=recv.at[r],
            device_id=target, device_id_type=MESH,
        )

    pending = []

    def start(src, dst, target, s, r, local=None):
        if local is True:
            pltpu.make_async_copy(src, dst, recv.at[r]).start()
            return
        copy = remote(src, dst, target, s, r)
        if local is None:
            copy.start()
            pending.append((None, copy))
            return
        pl.when(jnp.logical_not(local))(copy.start)
        pl.when(local)(pltpu.make_async_copy(src, dst, recv.at[r]).start)
        pending.append((jnp.logical_not(local), copy))

    def arrived(dst, r):
        remote(dst, dst, (row, col), 0, r).wait_recv()

    partner = device(x, y, z0, zh, 1 - core)

    a_load = pltpu.make_async_copy(a_hbm, a_ref, load)
    a_load.start()
    own_noise[...] = jnp.broadcast_to(q_ref[...], own_noise.shape)

    mine = x // 2 == core
    part = x % 2

    def strip_target(h):
        return device(core + 2 * h, y, z0, zh, x // 2), mine & (core + 2 * h == x)

    for cc in range(2):
        for h in range(2):
            target, local = strip_target(h)
            start(
                p_ref.at[:, pl.ds(TILE * h + HALF * cc, HALF)],
                ext_p.at[cc, pl.ds(pl.multiple_of(2 * TILE + HALF * part, HALF), HALF), :],
                target, S_RELAYOUT + 2 * cc + h, R_RELAYOUT + 2 * cc + part, local,
            )

    for h in range(2):
        target, local = strip_target(h)
        start(own_noise, noise.at[part], target, S_NOISE + h, R_NOISE + part, local)

    def right(x):
        return (x + 1) % 4

    def left(x):
        return (x + 3) % 4

    def split_band(c):
        for b in range(2):
            empty = slice(0, BS) if b else slice(WIDTH * BS, SPAN)
            rows = slice(b * BS, (b + 1) * BS)
            band_hi[c, rows, empty] = jnp.zeros((BS, BS), BF16)
            band_lo[c, rows, empty] = jnp.zeros((BS, BS), BF16)
            for d in range(WIDTH):
                value = band[c, b, :, d * BS:(d + 1) * BS]
                hi = value.astype(BF16)
                cols = slice((b + d) * BS, (b + d + 1) * BS)
                band_hi[c, rows, cols] = hi
                band_lo[c, rows, cols] = (value - hi.astype(F32)).astype(BF16)

    def block(b, d):
        wanted, slot = 2 * row + b + d - REACH, -1
        for s in range(pattern_ref.shape[1]):
            slot = jnp.where(pattern_ref[b, s] == wanted, s, slot)
        slot = jnp.where(wanted >= 0, slot, -1)
        return jnp.where(slot >= 0, a_ref[b, jnp.maximum(slot, 0)], 0.0)

    a_load.wait()
    for d in range(WIDTH):
        strip[:, d * BS:(d + 1) * BS] = block(core, d)
    for t, near_x in enumerate((right(x), left(x))):
        start(strip, band.at[part, core], device(near_x, y, z0, zh, x // 2),
              S_BAND + t, R_BAND + 2 * part + core)

    @pl.when(mine)
    def _():
        for b in range(2):
            for d in range(WIDTH):
                band[part, b, :, d * BS:(d + 1) * BS] = block(b, d)
        split_band(part)

    step = (x + 4 - 2 * core) % 4
    fwd_c = 1 - step % 2
    fwd_right = jnp.logical_or(step == 1, step == 2)
    fwd_b = jnp.where(fwd_right, 0, 1)
    fwd_x = jnp.where(fwd_right, right(x), left(x))

    def forward_band():
        unit = band.at[fwd_c, fwd_b]
        arrived(unit, R_BAND + 2 * fwd_c + fwd_b)
        fwd_copy.start()

    fwd_copy = remote(band.at[fwd_c, fwd_b], band.at[fwd_c, fwd_b],
                      device(fwd_x, y, z0, zh, core), S_FWD, R_BAND + 2 * fwd_c + fwd_b)
    pending.append((None, fwd_copy))

    d_slot = jnp.where(z0 == 0, 4, 0)
    y_slot = 4 - d_slot
    y_next = jnp.where(z0 == 0, (y + 1) % 4, (y + 3) % 4)
    near = jnp.where(core == 0, 1, 3)
    f_slot = jnp.where(core == 0, 4, 0)
    f_dst = jnp.where(core == 0, 3, 1)
    f_from_z = f_slot == d_slot

    def halo(ext, base):
        def at(v, slot):
            return ext.at[v // 2, pl.ds(pl.multiple_of(slot * TILE + HALF * (v % 2), HALF), HALF), :]

        def sem(kind, v):
            return 16 * base + 4 * kind + v

        def own(v):
            start(at(v, 2), at(v, y_slot), device(x, y, 1 - z0, zh, core),
                  S_HALO + sem(0, v), R_HALO + sem(0, v))
            start(at(v, 2), at(v, near), partner, S_HALO + sem(1, v), R_HALO + sem(1, v))

        def across(v):
            return remote(at(v, f_slot), at(v, f_dst), partner,
                          S_HALO + sem(3, v), R_HALO + sem(3, v))

        def from_z(v):
            arrived(at(v, d_slot), R_HALO + sem(0, v))
            start(at(v, d_slot), at(v, y_slot), device(x, y_next, z0, zh, core),
                  S_HALO + sem(2, v), R_HALO + sem(2, v))
            pl.when(f_from_z)(lambda: across(v).start())

        def from_y(v):
            arrived(at(v, y_slot), R_HALO + sem(2, v))
            pl.when(jnp.logical_not(f_from_z))(lambda: across(v).start())
            pending.append((None, across(v)))

        def rest(v):
            arrived(at(v, 4 - near), R_HALO + sem(1, v))
            arrived(at(v, 4 - f_dst), R_HALO + sem(3, v))

        return own, from_z, from_y, rest

    def split(ext, cc):
        def piece(n, _):
            rows = pl.ds(pl.multiple_of(n * BS, BS), BS)
            value = ext[cc, rows, :]
            hi = value.astype(BF16)
            ext_hi[cc, rows, :] = hi
            ext_lo[cc, rows, :] = (value - hi.astype(F32)).astype(BF16)
            return 0
        lax.fori_loop(0, 5 * TILE // BS, piece, 0)

    def product(c, cc):
        rows = pl.ds(pl.multiple_of(HALF * c, HALF), SPAN)
        hi, lo = ext_hi[cc, rows, :], ext_lo[cc, rows, :]
        acc = jnp.dot(band_hi[c], hi, preferred_element_type=F32)
        acc += jnp.dot(band_hi[c], lo, preferred_element_type=F32)
        acc += jnp.dot(band_lo[c], hi, preferred_element_type=F32)
        return acc

    def mirror(base, src, mid, dst):
        def quarter(ref, c, d, n):
            return ref.at[c, d, pl.ds(pl.multiple_of(n * QUARTER, QUARTER), QUARTER), :]

        def spread(c, d):
            base_s, base_r = S_MIRROR + 32 * base + 16 * c + 8 * d, R_MIRROR + 32 * base + 16 * c + 8 * d
            for n in (1, 3, 2, 0):
                r = (y + n) % 4
                start(quarter(src, c, d, r), quarter(mid, c, d, y), device(x, r, z0, zh, core),
                      base_s + n, base_r + y, None if n else True)

        def onward(c, d):
            base_s, base_r = S_MIRROR + 32 * base + 16 * c + 8 * d, R_MIRROR + 32 * base + 16 * c + 8 * d
            for n in (0, 1, 3, 2):
                r = (y + n) % 4
                unit = quarter(mid, c, d, r)
                arrived(unit, base_r + r)
                here = (x == z0 + 2 * core) & (y == zh) & (z0 == part) & (zh == r) & mine
                start(unit, quarter(dst, c, d, y), device(z0 + 2 * core, zh, part, r, x // 2),
                      base_s + 4 + n, base_r + 4 + y, here)

        def landed(c, d):
            for r in range(4):
                arrived(quarter(dst, c, d, r), R_MIRROR + 32 * base + 16 * c + 8 * d + 4 + r)

        return spread, onward, landed

    on_diagonal = tile_i == tile_j
    eye = (
        lax.broadcasted_iota(jnp.int32, (HALF, HALF), 0)
        == lax.broadcasted_iota(jnp.int32, (HALF, HALF), 1)
    )

    def diagonal(c):
        values = jnp.broadcast_to(noise[c, 0:1, :], (HALF, HALF))
        return jnp.where(jnp.logical_and(eye, on_diagonal), values, 0.0)

    own, from_z, from_y, rest = halo(ext_p, 0)
    for v in range(4):
        arrived(ext_p.at[v // 2, pl.ds(2 * TILE + HALF * (v % 2), HALF), :], R_RELAYOUT + v)
        own(v)
    for n in range(5):
        if n < 4:
            from_z(n)
        if n > 0:
            from_y(n - 1)
    for cc in range(2):
        rest(2 * cc)
        rest(2 * cc + 1)
        split(ext_p, cc)
    for c in range(2):
        arrived(noise.at[c], R_NOISE + c)

    spread, onward, landed = mirror(0, first, first_m, first_t)
    other = jnp.logical_not(mine)
    soon = jnp.where((step == 1) | (step == 2), 1, 0)
    late = 1 - soon

    @pl.when(other)
    def _():
        forward_band()
        arrived(band.at[soon, 1 - fwd_b], R_BAND + 2 * soon + 1 - fwd_b)
        split_band(soon)

    for cc in range(2):
        first[soon, cc] = product(soon, cc)
        spread(soon, cc)
    pl.when(mine)(forward_band)
    onward(soon, 0)
    onward(soon, 1)
    pl.when(other)(lambda: arrived(band.at[late, fwd_b], R_BAND + 2 * late + fwd_b))
    arrived(band.at[late, 1 - fwd_b], R_BAND + 2 * late + 1 - fwd_b)
    split_band(late)
    for cc in range(2):
        first[late, cc] = product(late, cc)
        spread(late, cc)
    onward(late, 0)
    onward(late, 1)

    own, from_z, from_y, rest = halo(ext_k, 1)

    def combine(cc):
        for c in range(2):
            landed(cc, c)
            k = first[c, cc] + first_t[cc, c].T
            if c == cc:
                k += diagonal(c)
            ext_k[cc, 2 * TILE + HALF * c:2 * TILE + HALF * (c + 1), :] = k
            own(2 * cc + c)

    spread, onward, landed_total = mirror(1, total, total_m, total_t)

    def apply(cc):
        rest(2 * cc)
        rest(2 * cc + 1)
        split(ext_k, cc)
        for c in range(2):
            total[cc, c] = 0.25 * first[c, cc] + 0.03125 * product(c, cc)
            spread(cc, c)

    combine(0)
    from_z(0)
    from_z(1)
    combine(1)
    from_y(0)
    from_z(2)
    from_y(1)
    from_z(3)
    apply(0)
    from_y(2)
    from_y(3)
    onward(0, 0)
    onward(0, 1)
    apply(1)
    onward(1, 0)
    onward(1, 1)

    for c in range(2):
        target = device(2 * core + c, y, z0, zh, part)
        local = (2 * core + c == x) & (part == core)
        for cc in range(2):
            landed_total(c, cc)
            p = ext_p[cc, 2 * TILE + HALF * c:2 * TILE + HALF * (c + 1), :]
            value = p + (total[cc, c] + total_t[c, cc].T)
            if c == cc:
                value += 0.25 * diagonal(c)
            result[c, cc] = value
            start(
                result.at[c, cc],
                o_ref.at[:, pl.ds(pl.multiple_of(TILE * (x // 2) + HALF * cc, HALF), HALF)],
                target, S_BACK + 2 * c + cc, R_BACK + 2 * (x // 2) + cc, local,
            )
    for h in range(2):
        for cc in range(2):
            arrived(o_ref.at[:, pl.ds(TILE * h + HALF * cc, HALF)], R_BACK + 2 * h + cc)

    for condition, copy in pending:
        if condition is None:
            copy.wait_send()
        else:
            pl.when(condition)(copy.wait_send)


def body(p_cov, a_blocks, pattern, q_diag):
    vmem = pl.BlockSpec(memory_space=pltpu.VMEM)
    return pl.pallas_call(
        kernel,
        out_shape=jax.ShapeDtypeStruct(p_cov.shape, F32),
        in_specs=[
            pl.BlockSpec(memory_space=pltpu.SMEM),
            pl.BlockSpec(memory_space=pl.ANY),
            pl.BlockSpec(memory_space=pl.ANY),
            vmem,
        ],
        out_specs=vmem,
        scratch_shapes=[
            pltpu.VMEM(a_blocks.shape, F32),
            pltpu.VMEM((8, HALF), F32),
            pltpu.VMEM((BS, WIDTH * BS), F32),
            pltpu.VMEM((2, 2, BS, WIDTH * BS), F32),
            pltpu.VMEM((2, HALF, SPAN), BF16),
            pltpu.VMEM((2, HALF, SPAN), BF16),
            pltpu.VMEM((2, 5 * TILE, HALF), F32),
            pltpu.VMEM((2, 5 * TILE, HALF), F32),
            pltpu.VMEM((2, 5 * TILE, HALF), BF16),
            pltpu.VMEM((2, 5 * TILE, HALF), BF16),
            *[pltpu.VMEM((2, 2, HALF, HALF), F32)] * 7,
            pltpu.VMEM((2, 8, HALF), F32),
            pltpu.SemaphoreType.DMA((N_SEND,)),
            pltpu.SemaphoreType.DMA((N_RECV,)),
            pltpu.SemaphoreType.DMA(()),
        ],
        compiler_params=pltpu.CompilerParams(has_side_effects=True, vmem_limit_bytes=60 * 1024 * 1024),
    )(pattern, p_cov, a_blocks, q_diag.reshape(1, HALF))


def solution(mesh):
    return jax.shard_map(
        body,
        mesh=mesh,
        in_specs=(P("row", "col"), P("row", None, None, None), P("row", None), P("row")),
        out_specs=P("row", "col"),
        check_vma=False,
    )
```

time: 201 us -> 174 us (0.87)
  Pallas kernels: 196 us -> 170 us
    pallas_call x1, Pallas kernels: 196 us -> 170 us  [body(): pl.pallas_call(kernel, out_shape=jax.ShapeDtypeStruct(p_cov.shape, F32),...]
where the time goes in v3:
time: 174 us; the launch traced here: 172 us
  Pallas kernels  170 us (98%)
  local copies, waits for them, and re-layouts  2.31 us (1%)
    pallas_call x1, Pallas kernels, body(): pl.pallas_call(kernel, out_shape=jax.ShapeDtypeStruct(p_cov.shape, F32),...  170 us

profile of v3, /device:TPU:27, one launch (start us, length us, event | category | flops | bytes accessed | tf_op | source)
XLA Modules:
  0.0 172.2 jit_solution(11920829803992557289)
XLA Ops:
  0.0 169.9 %shard_map.46 = f32[256,1024]{1,0:T(8,128)} custom-call(s32[2,16]{1,0:T(2,128)} %pattern_ref.1, f32[256,1024]{1,0:T(8,128)} %p_ref.1, f32[2,16,128,128]{3,2,1,0:T(8,128)} %a_hbm.1, f32[1,256]{1,0:T(1,128)} %bitcast.1), custom_call_target="tpu_custom_call" | custom-call | tf_op jit(solution)/shard_map/pallas_call | solution.py:345
  169.9 2.3 %copy.6 = f32[256,1024]{1,0:T(8,128)} copy(f32[256,1024]{1,0:T(8,128)} %shard_map.46) | data formatting | bytes 2097152

commit v4 on v3

--- a/solution.py
+++ b/solution.py
@@ -29,7 +29,8 @@
     col = lax.axis_index("col")
     x, z0, y = row % 4, (row // 4) % 2, row // 8
     core, zh = col % 2, col // 2
-    tile_i, tile_j = 4 * y + 2 * z0 + core, 4 * zh + 2 * (x % 2) + x // 2
+    j1 = (x + zh) % 2
+    tile_i, tile_j = 4 * y + 2 * z0 + core, 4 * zh + 2 * j1 + x // 2
 
     def device(x, y, z0, zh, core):
         return (8 * y + 4 * z0 + x, 2 * zh + core)
@@ -68,7 +69,8 @@
     part = x % 2
 
     def strip_target(h):
-        return device(core + 2 * h, y, z0, zh, x // 2), mine & (core + 2 * h == x)
+        x_to = (core + zh) % 2 + 2 * h
+        return device(x_to, y, z0, zh, x // 2), mine & (x_to == x)
 
     for cc in range(2):
         for h in range(2):
@@ -214,8 +216,9 @@
                 r = (y + n) % 4
                 unit = quarter(mid, c, d, r)
                 arrived(unit, base_r + r)
-                here = (x == z0 + 2 * core) & (y == zh) & (z0 == part) & (zh == r) & mine
-                start(unit, quarter(dst, c, d, y), device(z0 + 2 * core, zh, part, r, x // 2),
+                x_to = (z0 + r) % 2 + 2 * core
+                here = (x == x_to) & (y == zh) & (z0 == j1) & (zh == r) & mine
+                start(unit, quarter(dst, c, d, y), device(x_to, zh, j1, r, x // 2),
                       base_s + 4 + n, base_r + 4 + y, here)
 
         def landed(c, d):
@@ -315,8 +318,8 @@
     onward(1, 1)
 
     for c in range(2):
-        target = device(2 * core + c, y, z0, zh, part)
-        local = (2 * core + c == x) & (part == core)
+        target = device(2 * core + c, y, z0, zh, j1)
+        local = (2 * core + c == x) & (j1 == core)
         for cc in range(2):
             landed_total(c, cc)
             p = ext_p[cc, 2 * TILE + HALF * c:2 * TILE + HALF * (c + 1), :]

time: 174 us -> 172 us (0.989)
  the two profiles are of different devices: /device:TPU:27 before, /device:TPU:58 now
where the time goes in v4:
time: 172 us
  Pallas kernels  170 us (99%)
  local copies, waits for them, and re-layouts  2.31 us (1%)
    pallas_call x1, Pallas kernels, body(): pl.pallas_call(kernel, out_shape=jax.ShapeDtypeStruct(p_cov.shape, F32),...  170 us

profile of v4, /device:TPU:58, one launch (start us, length us, event | category | flops | bytes accessed | tf_op | source)
XLA Modules:
  0.0 171.9 jit_solution(13424873619278801873)
XLA Ops:
  0.0 169.6 %shard_map.46 = f32[256,1024]{1,0:T(8,128)} custom-call(s32[2,16]{1,0:T(2,128)} %pattern_ref.1, f32[256,1024]{1,0:T(8,128)} %p_ref.1, f32[2,16,128,128]{3,2,1,0:T(8,128)} %a_hbm.1, f32[1,256]{1,0:T(1,128)} %bitcast.1), custom_call_target="tpu_custom_call" | custom-call | tf_op jit(solution)/shard_map/pallas_call | solution.py:348
  169.6 2.3 %copy.6 = f32[256,1024]{1,0:T(8,128)} copy(f32[256,1024]{1,0:T(8,128)} %shard_map.46) | data formatting | bytes 2097152

commit v5 on v4

--- a/solution.py
+++ b/solution.py
@@ -301,15 +301,12 @@
             spread(cc, c)
 
     combine(0)
-    from_z(0)
-    from_z(1)
     combine(1)
-    from_y(0)
-    from_z(2)
-    from_y(1)
-    from_z(3)
+    for n in range(4):
+        from_z(n)
+        if n > 0:
+            from_y(n - 1)
     apply(0)
-    from_y(2)
     from_y(3)
     onward(0, 0)
     onward(0, 1)

time: 172 us -> 170 us (0.988)
  the two profiles are of different devices: /device:TPU:58 before, /device:TPU:27 now
where the time goes in v5:
time: 170 us; the launch traced here: 168 us
  Pallas kernels  166 us (98%)
  local copies, waits for them, and re-layouts  2.31 us (1%)
    pallas_call x1, Pallas kernels, body(): pl.pallas_call(kernel, out_shape=jax.ShapeDtypeStruct(p_cov.shape, F32),...  166 us

profile of v5, /device:TPU:27, one launch (start us, length us, event | category | flops | bytes accessed | tf_op | source)
XLA Modules:
  0.0 168.5 jit_solution(16156939773280003563)
XLA Ops:
  0.0 166.2 %shard_map.46 = f32[256,1024]{1,0:T(8,128)} custom-call(s32[2,16]{1,0:T(2,128)} %pattern_ref.1, f32[256,1024]{1,0:T(8,128)} %p_ref.1, f32[2,16,128,128]{3,2,1,0:T(8,128)} %a_hbm.1, f32[1,256]{1,0:T(1,128)} %bitcast.1), custom_call_target="tpu_custom_call" | custom-call | tf_op jit(solution)/shard_map/pallas_call | solution.py:345
  166.2 2.3 %copy.6 = f32[256,1024]{1,0:T(8,128)} copy(f32[256,1024]{1,0:T(8,128)} %shard_map.46) | data formatting | bytes 2097152

commit v6 on v5

--- a/solution.py
+++ b/solution.py
@@ -205,7 +205,7 @@
 
         def spread(c, d):
             base_s, base_r = S_MIRROR + 32 * base + 16 * c + 8 * d, R_MIRROR + 32 * base + 16 * c + 8 * d
-            for n in (1, 3, 2, 0):
+            for n in (0, 1, 3, 2):
                 r = (y + n) % 4
                 start(quarter(src, c, d, r), quarter(mid, c, d, y), device(x, r, z0, zh, core),
                       base_s + n, base_r + y, None if n else True)
@@ -351,7 +351,7 @@
             pl.BlockSpec(memory_space=pl.ANY),
             vmem,
         ],
-        out_specs=vmem,
+        out_specs=pl.BlockSpec(memory_space=pl.ANY),
         scratch_shapes=[
             pltpu.VMEM(a_blocks.shape, F32),
             pltpu.VMEM((8, HALF), F32),

time: 170 us -> 170 us (level)
  no operation moved by 1% of the time
where the time goes in v6:
time: 170 us; the launch traced here: 167 us
  Pallas kernels  165 us (97%)
  local copies, waits for them, and re-layouts  2.31 us (1%)
    pallas_call x1, Pallas kernels, body(): pl.pallas_call(kernel, out_shape=jax.ShapeDtypeStruct(p_cov.shape, F32),...  165 us

profile of v6, /device:TPU:27, one launch (start us, length us, event | category | flops | bytes accessed | tf_op | source)
XLA Modules:
  0.0 167.3 jit_solution(13027525480463539777)
XLA Ops:
  0.0 164.9 %shard_map.46 = f32[256,1024]{1,0:T(8,128)} custom-call(s32[2,16]{1,0:T(2,128)} %pattern_ref.1, f32[256,1024]{1,0:T(8,128)} %p_ref.1, f32[2,16,128,128]{3,2,1,0:T(8,128)} %a_hbm.1, f32[1,256]{1,0:T(1,128)} %bitcast.1), custom_call_target="tpu_custom_call" | custom-call | tf_op jit(solution)/shard_map/pallas_call | solution.py:345
  164.9 2.3 %copy.6 = f32[256,1024]{1,0:T(8,128)} copy(f32[256,1024]{1,0:T(8,128)} %shard_map.46) | data formatting | bytes 2097152
